TPU v7x, 512 devices: a whole 4x8x8 slice. The times are simulated.
512 devices in a mesh: box: 64 (over y, x, core), samp: 8 (over z).
Axes of the slice: x: 4, y: 8, z: 8, core: 2. Of those that a mesh axis runs over, the one named last changes fastest.
Arguments:
- currents: bfloat16 [2048, 8, 128], P(('box', 'samp')), may hold values from -6 to 6
- radiation: bfloat16 [2048, 2, 2, 512, 128], P(('box', 'samp')), may hold values from -0.1875 to 0.1875
- near_blocks: bfloat16 [2048, 8, 2, 128, 128], P(('box', 'samp')), may hold values from -0.125 to 0.125
- near_src: int32 [2048, 8], P(('box', 'samp')), may hold values from 0 to 2047, as said below
- leaf_parent: int32 [2048], P('box'), may hold values from 0 to 1023, as said below
- leaf_shift: int32 [2048], P('box'), may hold values from 0 to 7
- shift_table: bfloat16 [8, 2, 8192], P(None, None, 'samp'), may hold values from -4 to 4
- interp_idx: int32 [64, 2], P('samp'), may hold values from 0 to 3, as said below
- interp_val: bfloat16 [64, 2, 128, 128], P('samp'), may hold values from -0.375 to 0.375
- top_src: int32 [1024, 16], P('box'), may hold values from 0 to 1023, as said below
- top_disp: int32 [1024, 16], P('box'), may hold values from 0 to 31
- trans_table: bfloat16 [32, 2, 8192], P(None, None, 'samp'), may hold values from -1 to 1
Outputs:
- matvec: float32 [2048, 8, 128], P(('box', 'samp'))
Inputs may be any that keep to these rules, and one draw needn't show every extreme that they name: `near_src`: entry 0 of a leaf's row is the leaf itself; every entry lies in the 4 leaves of the leaf's own device or of the devices just before and after it in box+samp order (leaves numbered box-major), and these ends are reached. `leaf_parent`: the parent of leaf l lies in its box group: its value divided by 16 equals l divided by 32. `interp_idx`: the 2 entries of a row differ. `top_src`: a source of top box t is another box of t's group (t // 16), or one of the last 8 boxes of the group before it, or one of the first 8 boxes of the group after it; both rims are reached.
All inputs are finite; a program needn't handle non-finite values.
Results may differ from a plain program's by a relative error of at most 0.013.
Values may be sent and summed in bfloat16 or wider, within the bound.
A program may use at most 64 MiB of HBM per device.

v0:
```python
import jax
import jax.numpy as jnp
from jax import lax
from jax.sharding import PartitionSpec as P

HIGHEST = lax.Precision.HIGHEST


def with_halo(cells, sides, width):
    for axis, dim in sides:
        count = lax.axis_size(axis)
        ends = count - 1
        head = lax.slice_in_dim(cells, 0, width, axis=dim)
        tail = lax.slice_in_dim(cells, cells.shape[dim] - width, cells.shape[dim], axis=dim)
        cells = jnp.concatenate(
            [
                lax.ppermute(tail, axis, [(i, (i + 1) % count) for i in range(ends)]),
                cells,
                lax.ppermute(head, axis, [((i + 1) % count, i) for i in range(ends)]),
            ],
            axis=dim,
        )
    return cells


def complex_mul(a_real, a_imag, b_real, b_imag):
    return (a_real * b_real - a_imag * b_imag, a_real * b_imag + a_imag * b_real)


def contract(form, first_op, second_op):
    return jnp.einsum(form, first_op, second_op, preferred_element_type=jnp.float32)


def per_device(
    currents,
    radiation,
    near_blocks,
    near_src,
    leaf_parent,
    leaf_shift,
    shift_table,
    interp_idx,
    interp_val,
    top_src,
    top_disp,
    trans_table,
):
    leaf_count = currents.shape[0]
    half_comp = currents.shape[1]
    excite = half_comp // 2
    comps = 2 * half_comp
    samp_count = lax.axis_size("samp")
    group_index = lax.axis_index("box")
    first_leaf = (group_index * samp_count + lax.axis_index("samp")) * leaf_count
    top_count = top_src.shape[0]
    block_size = interp_val.shape[2]
    leaf_samples = radiation.shape[3]
    in_blocks = leaf_samples // block_size
    local_blocks = interp_val.shape[0]
    local_samples = local_blocks * block_size
    neighbours = with_halo(currents, ((("box", "samp"), 0),), leaf_count)
    rad_real = radiation[:, :, 0]
    rad_imag = radiation[:, :, 1]
    form_out = "lpqu,leu->lpeq"
    out_real = contract(form_out, rad_real, currents[:, :excite]) - contract(
        form_out, rad_imag, currents[:, excite:]
    )
    out_imag = contract(form_out, rad_real, currents[:, excite:]) + contract(
        form_out, rad_imag, currents[:, :excite]
    )
    patterns = jnp.concatenate(
        [
            out_real.reshape(leaf_count, half_comp, leaf_samples),
            out_imag.reshape(leaf_count, half_comp, leaf_samples),
        ],
        axis=1,
    ).astype(jnp.bfloat16)
    piece = lax.all_gather(patterns, "samp", axis=0, tiled=True)
    piece_rows = piece.shape[0]
    picked = piece.reshape(piece_rows, comps, in_blocks, block_size)[:, :, interp_idx, :]
    moved_rows = contract("lcbri,brki->lcbk", picked, interp_val)
    moved = moved_rows.reshape(piece_rows, comps, local_samples)
    shift_onehot = (leaf_shift[:, None] == jnp.arange(shift_table.shape[0])[None, :]).astype(
        jnp.bfloat16
    )
    shift_rows = contract("ln,nrk->lrk", shift_onehot, shift_table)
    shift_real = shift_rows[:, 0:1]
    shift_imag = shift_rows[:, 1:2]
    up_real, up_imag = complex_mul(
        moved[:, :half_comp], moved[:, half_comp:], shift_real, shift_imag
    )
    shifted = jnp.concatenate([up_real, up_imag], axis=1)
    parent_local = leaf_parent - group_index * top_count
    member = parent_local[None, :] == jnp.arange(top_count)[:, None]
    top_patterns = jnp.einsum(
        "tl,lck->tck", member.astype(jnp.float32), shifted, precision=HIGHEST
    ).astype(jnp.bfloat16)
    padded = with_halo(top_patterns, (("box", 0),), top_count)
    base_index = group_index * top_count - top_count
    disp_count = trans_table.shape[0]

    def add_entry(entry, total):
        source_rows = jnp.take(padded, top_src[:, entry] - base_index, axis=0).astype(jnp.float32)
        disp_onehot = (top_disp[:, entry][:, None] == jnp.arange(disp_count)[None, :]).astype(
            jnp.bfloat16
        )
        coeff = contract("tn,nrk->trk", disp_onehot, trans_table)
        part_real, part_imag = complex_mul(
            coeff[:, 0:1], coeff[:, 1:2], source_rows[:, :half_comp], source_rows[:, half_comp:]
        )
        return total + jnp.concatenate([part_real, part_imag], axis=1)

    incoming = lax.fori_loop(
        0, top_src.shape[1], add_entry, jnp.zeros((top_count, comps, local_samples), jnp.float32)
    ).astype(jnp.bfloat16)
    spread = contract("tl,tck->lck", member.astype(jnp.bfloat16), incoming)
    down_real, down_imag = complex_mul(
        shift_real, -shift_imag, spread[:, :half_comp], spread[:, half_comp:]
    )
    down = jnp.concatenate([down_real, down_imag], axis=1).astype(jnp.bfloat16)
    block_onehot = (interp_idx[:, :, None] == jnp.arange(in_blocks)[None, None, :]).astype(
        jnp.float32
    )
    parts = contract(
        "lcbk,brki->lcbri",
        down.reshape(leaf_count * lax.axis_size("samp"), comps, local_blocks, block_size),
        interp_val,
    )
    folded = jnp.einsum("lcbri,brq->lcqi", parts, block_onehot, precision=HIGHEST)
    far = lax.psum_scatter(
        folded.reshape(leaf_count * lax.axis_size("samp"), comps, leaf_samples).astype(
            jnp.bfloat16
        ),
        "samp",
        scatter_dimension=0,
        tiled=True,
    )
    far_real = far[:, :half_comp].reshape(leaf_count, 2, excite, leaf_samples)
    far_imag = far[:, half_comp:].reshape(leaf_count, 2, excite, leaf_samples)
    form_back = "lpqu,lpeq->leu"
    recv_real = contract(form_back, rad_real, far_real) + contract(form_back, rad_imag, far_imag)
    recv_imag = contract(form_back, rad_real, far_imag) - contract(form_back, rad_imag, far_real)
    near_rows = jnp.take(neighbours, near_src - first_leaf + leaf_count, axis=0)
    block_real = near_blocks[:, :, 0]
    block_imag = near_blocks[:, :, 1]
    form_near = "lnuv,lnev->leu"
    near_real = contract(form_near, block_real, near_rows[:, :, :excite]) - contract(
        form_near, block_imag, near_rows[:, :, excite:]
    )
    near_imag = contract(form_near, block_real, near_rows[:, :, excite:]) + contract(
        form_near, block_imag, near_rows[:, :, :excite]
    )
    return jnp.concatenate([recv_real + near_real, recv_imag + near_imag], axis=1)


def solution(mesh):
    placed = (
        P(("box", "samp"), None, None),
        P(("box", "samp"), None, None, None, None),
        P(("box", "samp"), None, None, None, None),
        P(("box", "samp"), None),
        P("box"),
        P("box"),
        P(None, None, "samp"),
        P("samp", None),
        P("samp", None, None, None),
        P("box", None),
        P("box", None),
        P(None, None, "samp"),
    )
    return jax.shard_map(
        per_device,
        mesh=mesh,
        in_specs=placed,
        out_specs=P(("box", "samp"), None, None),
        check_vma=False,
    )
```

profile of v0, /device:TPU:2, one launch (start us, length us, event | category | flops | bytes accessed | tf_op | source)
XLA Modules:
  0.0 176.0 jit_solution(13195029039709390717)
XLA Ops:
  6.6 1.8 %fusion.46 = f32[4,4,2,512]{3,1,2,0:T(4,128)S(1)} fusion(bf16[4,2,2,512,128]{4,3,2,1,0:T(8,128)(2,1)} %param.15, bf16[4,8,128]{2,1,0:T(8,128)(2,1)} %param.14), kind=kOutput, calls=%fused_computation.65 | convolution fusion | flops 4194304 | bytes 1118208 | tf_op jit(solution)/shard_map/lpqu,leu->lpeq/dot_general | solution.py:31
  8.4 1.6 fusion.44
  10.3 0.4 fusion.25
  10.7 0.4 fusion.24
  11.1 31.6 %all_gather.3 = bf16[32,16,512]{2,1,0:T(8,128)(2,1)S(1)} all-gather(bf16[4,16,512]{2,1,0:T(8,128)(2,1)S(1)} %pad_maximum_fusion.1), channel_id=1, replica_groups=mesh['box'=64,'samp'=8] {'samp'}, dimensions={0}, use_global_device_ids=true | all-gather | bytes 589824 | tf_op jit(solution)/shard_map/all_gather | solution.py:78
  43.1 1.1 gather_fusion.1
  44.2 0.7 convolution_bitcast_fusion.1
  44.9 2.5 %copy.92 = f32[32,16,8,128]{3,2,0,1:T(8,128)} copy(f32[32,16,8,128]{3,1,0,2:T(8,128)S(1)} %convolution_bitcast_fusion.1) | data formatting | bytes 4194304 | tf_op jit(solution)/shard_map/reshape | solution.py:82
  47.4 1.7 reshape.96
  49.5 0.8 fusion.16
  50.4 1.9 %collective-permute-start = (bf16[16,16,1024]{2,0,1:T(8,128)(2,1)S(1)}, bf16[16,16,1024]{2,0,1:T(8,128)(2,1)S(1)}, u32[]{:S(2)}, u32[]{:S(2)}) collective-permute-start(bf16[16,16,1024]{2,0,1:T(8,128)(2,1)S(1)} %fusion.16), channel_id=1, source_target_pairs={{0,8},{8,16},{16,24},{24,32},{32,40},{40,48},{48,56},{56,64},{64,7... | collective-permute-start | bytes 1572872 | tf_op jit(solution)/shard_map/ppermute | solution.py:17
  52.3 3.8 %collective-permute-start.1 = (bf16[16,16,1024]{2,0,1:T(8,128)(2,1)S(1)}, bf16[16,16,1024]{2,0,1:T(8,128)(2,1)}, u32[]{:S(2)}, u32[]{:S(2)}) collective-permute-start(bf16[16,16,1024]{2,0,1:T(8,128)(2,1)S(1)} %fusion.16), channel_id=1, source_target_pairs={{8,0},{16,8},{24,16},{32,24},{40,32},{48,40},{56,48},{64,56},{72,6... | collective-permute-start | bytes 1572872 | tf_op jit(solution)/shard_map/ppermute | solution.py:19
  56.3 4.5 %collective-permute-done = bf16[16,16,1024]{2,0,1:T(8,128)(2,1)S(1)} collective-permute-done((bf16[16,16,1024]{2,0,1:T(8,128)(2,1)S(1)}, bf16[16,16,1024]{2,0,1:T(8,128)(2,1)S(1)}, u32[]{:S(2)}, u32[]{:S(2)}) %collective-permute-start) | collective-permute-done | bytes 524320 | tf_op jit(solution)/shard_map/ppermute | solution.py:17
  60.9 1.8 collective-permute-done.1
  62.6 1.2 pad_maximum_fusion
  63.8 2.0 %copy.70 = bf16[48,16,1024]{2,1,0:T(8,128)(2,1)} copy(bf16[48,16,1024]{2,0,1:T(8,128)(2,1)S(1)} %pad_maximum_fusion) | data formatting | bytes 3145728
  65.9 48.1 %while.14 = (s32[]{:T(128)}, f32[16,16,1024]{2,1,0:T(8,128)S(1)}, s32[16,16]{0,1:T(8,128)S(1)}, bf16[32,2,1024]{2,0,1:T(8,128)(2,1)S(1)}, s32[16,16]{0,1:T(8,128...) while((s32[]{:T(128)}, f32[16,16,1024]{2,1,0:T(8,128)S(1)}, ...), condition=%wide.region_1.0_spmd.clone, body=%wide.region_0.1_spmd.clone.sunk | while | flops 4195955 | bytes 8524371 | solution.py:113
  65.9 2.0 %gather_fusion = bf16[16,16,1024]{2,1,0:T(8,128)(2,1)S(1)} fusion(bf16[48,16,1024]{2,1,0:T(8,128)(2,1)} %get-tuple-element.292, s32[1024]{0:T(1024)S(1)} %pad_clamp_fusion.4), kind=kCustom, calls=%fused_computation.clone.clone.1 | custom fusion | bytes 1048640 | tf_op jit(solution)/shard_map/while/body/eval_jaxpr/jit(_take)/gather | solution.py:103
  68.5 0.3 maximum_add_fusion.2
  68.9 2.0 %gather_fusion = bf16[16,16,1024]{2,1,0:T(8,128)(2,1)S(1)} fusion(bf16[48,16,1024]{2,1,0:T(8,128)(2,1)} %get-tuple-element.292, s32[1024]{0:T(1024)S(1)} %pad_clamp_fusion.4), kind=kCustom, calls=%fused_computation.clone.clone.1 | custom fusion | bytes 1048640 | tf_op jit(solution)/shard_map/while/body/eval_jaxpr/jit(_take)/gather | solution.py:103
  71.5 0.3 maximum_add_fusion.2
  71.9 2.0 %gather_fusion = bf16[16,16,1024]{2,1,0:T(8,128)(2,1)S(1)} fusion(bf16[48,16,1024]{2,1,0:T(8,128)(2,1)} %get-tuple-element.292, s32[1024]{0:T(1024)S(1)} %pad_clamp_fusion.4), kind=kCustom, calls=%fused_computation.clone.clone.1 | custom fusion | bytes 1048640 | tf_op jit(solution)/shard_map/while/body/eval_jaxpr/jit(_take)/gather | solution.py:103
  74.5 0.3 maximum_add_fusion.2
  74.9 2.0 %gather_fusion = bf16[16,16,1024]{2,1,0:T(8,128)(2,1)S(1)} fusion(bf16[48,16,1024]{2,1,0:T(8,128)(2,1)} %get-tuple-element.292, s32[1024]{0:T(1024)S(1)} %pad_clamp_fusion.4), kind=kCustom, calls=%fused_computation.clone.clone.1 | custom fusion | bytes 1048640 | tf_op jit(solution)/shard_map/while/body/eval_jaxpr/jit(_take)/gather | solution.py:103
  77.5 0.3 maximum_add_fusion.2
  77.9 2.0 %gather_fusion = bf16[16,16,1024]{2,1,0:T(8,128)(2,1)S(1)} fusion(bf16[48,16,1024]{2,1,0:T(8,128)(2,1)} %get-tuple-element.292, s32[1024]{0:T(1024)S(1)} %pad_clamp_fusion.4), kind=kCustom, calls=%fused_computation.clone.clone.1 | custom fusion | bytes 1048640 | tf_op jit(solution)/shard_map/while/body/eval_jaxpr/jit(_take)/gather | solution.py:103
  80.5 0.3 maximum_add_fusion.2
  80.9 2.0 %gather_fusion = bf16[16,16,1024]{2,1,0:T(8,128)(2,1)S(1)} fusion(bf16[48,16,1024]{2,1,0:T(8,128)(2,1)} %get-tuple-element.292, s32[1024]{0:T(1024)S(1)} %pad_clamp_fusion.4), kind=kCustom, calls=%fused_computation.clone.clone.1 | custom fusion | bytes 1048640 | tf_op jit(solution)/shard_map/while/body/eval_jaxpr/jit(_take)/gather | solution.py:103
  83.5 0.3 maximum_add_fusion.2
  83.9 2.0 %gather_fusion = bf16[16,16,1024]{2,1,0:T(8,128)(2,1)S(1)} fusion(bf16[48,16,1024]{2,1,0:T(8,128)(2,1)} %get-tuple-element.292, s32[1024]{0:T(1024)S(1)} %pad_clamp_fusion.4), kind=kCustom, calls=%fused_computation.clone.clone.1 | custom fusion | bytes 1048640 | tf_op jit(solution)/shard_map/while/body/eval_jaxpr/jit(_take)/gather | solution.py:103
  86.5 0.3 maximum_add_fusion.2
  86.9 2.0 %gather_fusion = bf16[16,16,1024]{2,1,0:T(8,128)(2,1)S(1)} fusion(bf16[48,16,1024]{2,1,0:T(8,128)(2,1)} %get-tuple-element.292, s32[1024]{0:T(1024)S(1)} %pad_clamp_fusion.4), kind=kCustom, calls=%fused_computation.clone.clone.1 | custom fusion | bytes 1048640 | tf_op jit(solution)/shard_map/while/body/eval_jaxpr/jit(_take)/gather | solution.py:103
  89.6 0.3 maximum_add_fusion.2
  90.0 2.0 %gather_fusion = bf16[16,16,1024]{2,1,0:T(8,128)(2,1)S(1)} fusion(bf16[48,16,1024]{2,1,0:T(8,128)(2,1)} %get-tuple-element.292, s32[1024]{0:T(1024)S(1)} %pad_clamp_fusion.4), kind=kCustom, calls=%fused_computation.clone.clone.1 | custom fusion | bytes 1048640 | tf_op jit(solution)/shard_map/while/body/eval_jaxpr/jit(_take)/gather | solution.py:103
  92.6 0.3 maximum_add_fusion.2
  93.0 2.0 %gather_fusion = bf16[16,16,1024]{2,1,0:T(8,128)(2,1)S(1)} fusion(bf16[48,16,1024]{2,1,0:T(8,128)(2,1)} %get-tuple-element.292, s32[1024]{0:T(1024)S(1)} %pad_clamp_fusion.4), kind=kCustom, calls=%fused_computation.clone.clone.1 | custom fusion | bytes 1048640 | tf_op jit(solution)/shard_map/while/body/eval_jaxpr/jit(_take)/gather | solution.py:103
  95.6 0.3 maximum_add_fusion.2
  96.0 2.0 %gather_fusion = bf16[16,16,1024]{2,1,0:T(8,128)(2,1)S(1)} fusion(bf16[48,16,1024]{2,1,0:T(8,128)(2,1)} %get-tuple-element.292, s32[1024]{0:T(1024)S(1)} %pad_clamp_fusion.4), kind=kCustom, calls=%fused_computation.clone.clone.1 | custom fusion | bytes 1048640 | tf_op jit(solution)/shard_map/while/body/eval_jaxpr/jit(_take)/gather | solution.py:103
  98.6 0.3 maximum_add_fusion.2
  99.0 2.0 %gather_fusion = bf16[16,16,1024]{2,1,0:T(8,128)(2,1)S(1)} fusion(bf16[48,16,1024]{2,1,0:T(8,128)(2,1)} %get-tuple-element.292, s32[1024]{0:T(1024)S(1)} %pad_clamp_fusion.4), kind=kCustom, calls=%fused_computation.clone.clone.1 | custom fusion | bytes 1048640 | tf_op jit(solution)/shard_map/while/body/eval_jaxpr/jit(_take)/gather | solution.py:103
  101.6 0.3 maximum_add_fusion.2
  102.0 2.0 %gather_fusion = bf16[16,16,1024]{2,1,0:T(8,128)(2,1)S(1)} fusion(bf16[48,16,1024]{2,1,0:T(8,128)(2,1)} %get-tuple-element.292, s32[1024]{0:T(1024)S(1)} %pad_clamp_fusion.4), kind=kCustom, calls=%fused_computation.clone.clone.1 | custom fusion | bytes 1048640 | tf_op jit(solution)/shard_map/while/body/eval_jaxpr/jit(_take)/gather | solution.py:103
  104.6 0.3 maximum_add_fusion.2
  105.0 2.0 %gather_fusion = bf16[16,16,1024]{2,1,0:T(8,128)(2,1)S(1)} fusion(bf16[48,16,1024]{2,1,0:T(8,128)(2,1)} %get-tuple-element.292, s32[1024]{0:T(1024)S(1)} %pad_clamp_fusion.4), kind=kCustom, calls=%fused_computation.clone.clone.1 | custom fusion | bytes 1048640 | tf_op jit(solution)/shard_map/while/body/eval_jaxpr/jit(_take)/gather | solution.py:103
  108.0 2.0 %gather_fusion = bf16[16,16,1024]{2,1,0:T(8,128)(2,1)S(1)} fusion(bf16[48,16,1024]{2,1,0:T(8,128)(2,1)} %get-tuple-element.292, s32[1024]{0:T(1024)S(1)} %pad_clamp_fusion.4), kind=kCustom, calls=%fused_computation.clone.clone.1 | custom fusion | bytes 1048640 | tf_op jit(solution)/shard_map/while/body/eval_jaxpr/jit(_take)/gather | solution.py:103
  110.6 0.3 maximum_add_fusion.2
  111.0 2.0 %gather_fusion = bf16[16,16,1024]{2,1,0:T(8,128)(2,1)S(1)} fusion(bf16[48,16,1024]{2,1,0:T(8,128)(2,1)} %get-tuple-element.292, s32[1024]{0:T(1024)S(1)} %pad_clamp_fusion.4), kind=kCustom, calls=%fused_computation.clone.clone.1 | custom fusion | bytes 1048640 | tf_op jit(solution)/shard_map/while/body/eval_jaxpr/jit(_take)/gather | solution.py:103
  113.6 0.3 maximum_add_fusion.2
  114.0 0.5 fusion.62
  115.8 0.7 convolution_bitcast_fusion
  116.5 4.0 %fusion.19 = bf16[32,16,4,128]{3,2,1,0:T(4,128)(2,1)S(1)} fusion(f32[32,16,8,2,128]{4,1,3,0,2:T(8,128)S(1)} %convolution_bitcast_fusion, s32[8,2]{0,1:T(2,128)S(1)} %copy-done.9), kind=kOutput, calls=%fused_computation.29 | convolution fusion | flops 50593856 | bytes 4718656 | tf_op jit(solution)/shard_map/lcbri,brq->lcqi/dot_general | solution.py:129
  120.6 1.0 convert_element_type.36
  121.6 3.7 %collective-permute-start.2 = (bf16[4,8,128]{2,1,0:T(8,128)(2,1)S(1)}, bf16[4,8,128]{2,1,0:T(8,128)(2,1)S(1)}, u32[]{:S(2)}, u32[]{:S(2)}) collective-permute-start(bf16[4,8,128]{2,1,0:T(8,128)(2,1)S(1)} %copy-done.4), channel_id=1, source_target_pairs={{0,1},{1,2},{2,3},{3,4},{4,5},{5,6},{6,7},{7,8},{8,9},{9,10},{10,1... | collective-permute-start | bytes 24584 | tf_op jit(solution)/shard_map/ppermute | solution.py:17
  125.3 4.6 %collective-permute-start.3 = (bf16[4,8,128]{2,1,0:T(8,128)(2,1)S(1)}, bf16[4,8,128]{2,1,0:T(8,128)(2,1)S(1)}, u32[]{:S(2)}, u32[]{:S(2)}) collective-permute-start(bf16[4,8,128]{2,1,0:T(8,128)(2,1)S(1)} %copy-done.4), channel_id=1, source_target_pairs={{1,0},{2,1},{3,2},{4,3},{5,4},{6,5},{7,6},{8,7},{9,8},{10,9},{11,1... | collective-permute-start | bytes 24584 | tf_op jit(solution)/shard_map/ppermute | solution.py:19
  130.0 1.2 collective-permute-done.3
  131.2 0.6 gather_fusion.2
  131.9 1.6 convolution_bitcast_fusion.7
  133.5 1.6 convolution_bitcast_fusion.3
  135.2 29.9 %reduce-scatter.2.cloned.1.call-done = bf16[4,16,512]{2,1,0:T(8,128)(2,1)} async-done(((bf16[32,16,512]{2,1,0:T(8,128)(2,1)}), bf16[4,16,512]{2,1,0:T(8,128)(2,1)}) %reduce-scatter.2.cloned.1.call-update) | async-done | bytes 65552 | tf_op jit(solution)/shard_map/reduce_scatter | solution.py:130
  165.0 0.8 fusion.91
  166.9 0.8 copy-done.3
  167.7 0.4 fusion.30
  168.1 0.4 fusion.27
  168.5 0.6 pad_maximum_fusion.3
  (174 shorter events, 13.6 us)
Async XLA Ops:
  6.5 37.6 %copy-start = (bf16[8,2,128,128]{3,2,1,0:T(8,128)(2,1)S(1)}, bf16[8,2,128,128]{3,2,1,0:T(8,128)(2,1)}, u32[]{:S(2)}) copy-start(bf16[8,2,128,128]{3,2,1,0:T(8,128)(2,1)} %param.22) | copy-start | bytes 1572868
  6.5 3.7 %copy-start.4 = (bf16[4,8,128]{2,1,0:T(8,128)(2,1)S(1)}, bf16[4,8,128]{2,1,0:T(8,128)(2,1)}, u32[]{:S(2)}) copy-start(bf16[4,8,128]{2,1,0:T(8,128)(2,1)} %param.14) | copy-start | bytes 24580
  6.5 3.7 %copy-start.1 = (bf16[4,2,2,512,128]{4,3,2,1,0:T(8,128)(2,1)S(1)}, bf16[4,2,2,512,128]{4,3,2,1,0:T(8,128)(2,1)}, u32[]{:S(2)}) copy-start(bf16[4,2,2,512,128]{4,3,2,1,0:T(8,128)(2,1)} %param.15) | copy-start | bytes 6291460
  6.5 3.4 %copy-start.11 = (s32[32]{0:T(128)S(1)}, s32[32]{0:T(128)}, u32[]{:S(2)}) copy-start(s32[32]{0:T(128)} %param.19) | copy-start | bytes 388
  6.5 3.4 %copy-start.6 = (bf16[8,2,1024]{2,1,0:T(2,128)(2,1)S(1)}, bf16[8,2,1024]{2,1,0:T(2,128)(2,1)}, u32[]{:S(2)}) copy-start(bf16[8,2,1024]{2,1,0:T(2,128)(2,1)} %param.20) | copy-start | bytes 98308
  6.5 158.5 %reduce-scatter.2.cloned.1.call-start = ((), (), s32[]{:S(2)}) async-start(), calls=%async_computation.1 | async-start | bytes 589824 | tf_op jit(solution)/shard_map/reduce_scatter | solution.py:130
  10.3 32.6 %copy-start.9 = (s32[8,2]{0,1:T(2,128)S(1)}, s32[8,2]{0,1:T(2,128)}, u32[]{:S(2)}) copy-start(s32[8,2]{0,1:T(2,128)} %param.21) | copy-start | bytes 196
  47.4 1.7 copy-start.12
  49.5 6.7 %copy-start.5 = (bf16[32,2,1024]{2,1,0:T(2,128)(2,1)S(1)}, bf16[32,2,1024]{2,1,0:T(2,128)(2,1)}, u32[]{:S(2)}) copy-start(bf16[32,2,1024]{2,1,0:T(2,128)(2,1)} %param.25) | copy-start | bytes 393220
  49.5 6.7 %copy-start.7 = (s32[16,16]{1,0:T(8,128)S(1)}, s32[16,16]{1,0:T(8,128)}, u32[]{:S(2)}) copy-start(s32[16,16]{1,0:T(8,128)} %param.24) | copy-start | bytes 3076
  49.5 6.8 %copy-start.8 = (s32[16,16]{1,0:T(8,128)S(1)}, s32[16,16]{1,0:T(8,128)}, u32[]{:S(2)}) copy-start(s32[16,16]{1,0:T(8,128)} %param.23) | copy-start | bytes 3076
  50.4 10.5 %collective-permute-start = (bf16[16,16,1024]{2,0,1:T(8,128)(2,1)S(1)}, bf16[16,16,1024]{2,0,1:T(8,128)(2,1)S(1)}, u32[]{:S(2)}, u32[]{:S(2)}) collective-permute-start(bf16[16,16,1024]{2,0,1:T(8,128)(2,1)S(1)} %fusion.16), channel_id=1, source_target_pairs={{0,8},{8,16},{16,24},{24,32},{32,40},{40,48},{48,56},{56,64},{64,7... | collective-permute-start | bytes 1572872 | tf_op jit(solution)/shard_map/ppermute | solution.py:17
  52.3 10.3 %collective-permute-start.1 = (bf16[16,16,1024]{2,0,1:T(8,128)(2,1)S(1)}, bf16[16,16,1024]{2,0,1:T(8,128)(2,1)}, u32[]{:S(2)}, u32[]{:S(2)}) collective-permute-start(bf16[16,16,1024]{2,0,1:T(8,128)(2,1)S(1)} %fusion.16), channel_id=1, source_target_pairs={{8,0},{16,8},{24,16},{32,24},{40,32},{48,40},{56,48},{64,56},{72,6... | collective-permute-start | bytes 1572872 | tf_op jit(solution)/shard_map/ppermute | solution.py:19
  116.5 13.4 %copy-start.10 = (s32[4,8]{1,0:T(4,128)S(1)}, s32[4,8]{1,0:T(4,128)}, u32[]{:S(2)}) copy-start(s32[4,8]{1,0:T(4,128)} %param.17) | copy-start | bytes 388
  120.6 45.3 %copy-start.2 = (bf16[4,2,2,512,128]{4,3,2,1,0:T(8,128)(2,1)S(1)}, bf16[4,2,2,512,128]{4,3,2,1,0:T(8,128)(2,1)}, u32[]{:S(2)}) copy-start(bf16[4,2,2,512,128]{4,3,2,1,0:T(8,128)(2,1)} %param.15) | copy-start | bytes 6291460
  121.6 8.4 %collective-permute-start.2 = (bf16[4,8,128]{2,1,0:T(8,128)(2,1)S(1)}, bf16[4,8,128]{2,1,0:T(8,128)(2,1)S(1)}, u32[]{:S(2)}, u32[]{:S(2)}) collective-permute-start(bf16[4,8,128]{2,1,0:T(8,128)(2,1)S(1)} %copy-done.4), channel_id=1, source_target_pairs={{0,1},{1,2},{2,3},{3,4},{4,5},{5,6},{6,7},{7,8},{8,9},{9,10},{10,1... | collective-permute-start | bytes 24584 | tf_op jit(solution)/shard_map/ppermute | solution.py:17
  125.3 5.9 %collective-permute-start.3 = (bf16[4,8,128]{2,1,0:T(8,128)(2,1)S(1)}, bf16[4,8,128]{2,1,0:T(8,128)(2,1)S(1)}, u32[]{:S(2)}, u32[]{:S(2)}) collective-permute-start(bf16[4,8,128]{2,1,0:T(8,128)(2,1)S(1)} %copy-done.4), channel_id=1, source_target_pairs={{1,0},{2,1},{3,2},{4,3},{5,4},{6,5},{7,6},{8,7},{9,8},{10,9},{11,1... | collective-permute-start | bytes 24584 | tf_op jit(solution)/shard_map/ppermute | solution.py:19
  166.1 1.6 copy-start.3
Sparse Core Ops, SparseCore 0:
  121.7 43.2 reduce-scatter.1
where the time goes:
time: 177 us; the launch traced here: 176 us
  local copies, waits for them, and re-layouts  44.3 us (25%)
  waiting for transfers between devices  37.4 us (21%)
  blocking collectives  31.6 us (18%)
  matrix products  19.5 us (11%)
  other arithmetic  14.1 us (8%)
  starting transfers between devices  14 us (8%)
  between operations  13.8 us (8%)
    gather x16, local copies, waits for them, and re-layouts, add_entry(): jnp.take(padded, top_src[:, entry] - base_index, axis=0).astype(jnp.float32)  31.8 us
    all_gather x1, blocking collectives, per_device(): piece = lax.all_gather(patterns, 'samp', axis=0, tiled=True)  31.6 us
    reduce_scatter x1, waiting for transfers between devices, per_device(): lax.psum_scatter(folded.reshape(leaf_count * lax.axis_size('samp'), comps...  29.9 us
    dot_general x32, matrix products, contract(): jnp.einsum(form, first_op, second_op, preferred_element_type=jnp.float32)  14.6 us
    ppermute x2, starting transfers between devices, with_halo(): lax.ppermute(head, axis, [((i + 1) % count, i) for i in range(ends)])  8.4 us
    ppermute x2, starting transfers between devices, with_halo(): lax.ppermute(tail, axis, [(i, (i + 1) % count) for i in range(ends)])  5.61 us
    add x16, other arithmetic, add_entry(): return total + jnp.concatenate([part_real, part_imag], axis=1)  5.52 us
    ppermute x2, waiting for transfers between devices, with_halo(): lax.ppermute(tail, axis, [(i, (i + 1) % count) for i in range(ends)])  4.53 us
  transfers between devices with their start and end apart: 5, of which 4 were waited for; matrix products, arithmetic and copies ran while one was open for 2% of the time, Pallas kernels for 0%

commit v1 on v0

--- a/solution.py
+++ b/solution.py
@@ -75,7 +75,9 @@
         ],
         axis=1,
     ).astype(jnp.bfloat16)
-    piece = lax.all_gather(patterns, "samp", axis=0, tiled=True)
+    piece = jnp.concatenate(
+        lax.all_to_all(jnp.stack([patterns] * lax.axis_size("samp")), "samp", 0, 0), axis=0
+    )
     piece_rows = piece.shape[0]
     picked = piece.reshape(piece_rows, comps, in_blocks, block_size)[:, :, interp_idx, :]
     moved_rows = contract("lcbri,brki->lcbk", picked, interp_val)

time: 177 us -> 172 us (0.972)
  blocking collectives: 31.6 us -> 0 us
  waiting for transfers between devices: 37.4 us -> 52.1 us
  starting transfers between devices: 14 us -> 23.8 us
    all_gather x1 -> x0, blocking collectives: 31.6 us -> none  [per_device(): piece = lax.all_gather(patterns, 'samp', axis=0, tiled=True)]
    all_to_all x0 -> x1, waiting for transfers between devices: none -> 16.5 us  [per_device(): lax.all_to_all(jnp.stack([patterns] * lax.axis_size('samp')), 'samp', 0, 0)]
    all_to_all x0 -> x1, starting transfers between devices: none -> 10.3 us  [per_device(): lax.all_to_all(jnp.stack([patterns] * lax.axis_size('samp')), 'samp', 0, 0)]
    unnamed x32 -> x34, local copies, waits for them, and re-layouts: 3.28 us -> 3.62 us
  transfers between devices with their start and end apart: 5 -> 6, of which waited for: 4 -> 5; matrix products, arithmetic and copies ran while one was open for 2% -> 3% of each run, Pallas kernels for 0% -> 0%
where the time goes in v1:
time: 172 us; the launch traced here: 171 us
  waiting for transfers between devices  52.1 us (30%)
  local copies, waits for them, and re-layouts  45.7 us (27%)
  starting transfers between devices  23.8 us (14%)
  matrix products  19.4 us (11%)
  other arithmetic  14.6 us (8%)
  between operations  13.8 us (8%)
    gather x16, local copies, waits for them, and re-layouts, add_entry(): jnp.take(padded, top_src[:, entry] - base_index, axis=0).astype(jnp.float32)  31.8 us
    reduce_scatter x1, waiting for transfers between devices, per_device(): lax.psum_scatter(folded.reshape(leaf_count * lax.axis_size('samp'), comps...  28.1 us
    all_to_all x1, waiting for transfers between devices, per_device(): lax.all_to_all(jnp.stack([patterns] * lax.axis_size('samp')), 'samp', 0, 0)  16.5 us
    dot_general x32, matrix products, contract(): jnp.einsum(form, first_op, second_op, preferred_element_type=jnp.float32)  14.6 us
    all_to_all x1, starting transfers between devices, per_device(): lax.all_to_all(jnp.stack([patterns] * lax.axis_size('samp')), 'samp', 0, 0)  10.3 us
    ppermute x2, starting transfers between devices, with_halo(): lax.ppermute(head, axis, [((i + 1) % count, i) for i in range(ends)])  9.01 us
    add x16, other arithmetic, add_entry(): return total + jnp.concatenate([part_real, part_imag], axis=1)  5.52 us
    ppermute x2, waiting for transfers between devices, with_halo(): lax.ppermute(tail, axis, [(i, (i + 1) % count) for i in range(ends)])  4.53 us
  transfers between devices with their start and end apart: 6, of which 5 were waited for; matrix products, arithmetic and copies ran while one was open for 3% of the time, Pallas kernels for 0%

profile of v1, /device:TPU:2, one launch (start us, length us, event | category | flops | bytes accessed | tf_op | source)
XLA Modules:
  0.0 170.6 jit_solution(17930255361013981896)
XLA Ops:
  6.5 1.8 %fusion.46 = f32[4,4,2,512]{3,1,2,0:T(4,128)S(1)} fusion(bf16[4,2,2,512,128]{4,3,2,1,0:T(8,128)(2,1)} %param.15, bf16[4,8,128]{2,1,0:T(8,128)(2,1)} %param.14), kind=kOutput, calls=%fused_computation.65 | convolution fusion | flops 4194304 | bytes 1118208 | tf_op jit(solution)/shard_map/lpqu,leu->lpeq/dot_general | solution.py:31
  8.3 1.6 fusion.44
  10.0 0.4 fusion.25
  10.4 0.4 fusion.24
  10.8 0.9 stack.2
  11.7 10.3 %all-to-all-start = ((bf16[8,4,16,512]{3,2,1,0:T(8,128)(2,1)}), bf16[8,4,16,512]{3,2,1,0:T(8,128)(2,1)S(1)}, u32[]{:S(2)}, u32[]{:S(2)}) async-start(bf16[8,4,16,512]{3,2,1,0:T(8,128)(2,1)} %stack.2), calls=%async_computation | async-start | bytes 1048576 | tf_op jit(solution)/shard_map/all_to_all | solution.py:79
  22.3 0.5 broadcast_subtract_fusion
  23.1 16.5 %all-to-all-done = bf16[8,4,16,512]{3,2,1,0:T(8,128)(2,1)S(1)} async-done(((bf16[8,4,16,512]{3,2,1,0:T(8,128)(2,1)}), bf16[8,4,16,512]{3,2,1,0:T(8,128)(2,1)S(1)}, u32[]{:S(2)}, u32[]{:S(2)}) %all-to-all-start) | async-done | bytes 524320 | tf_op jit(solution)/shard_map/all_to_all | solution.py:79
  39.7 1.1 gather_fusion.1
  40.8 0.7 convolution_bitcast_fusion.1
  41.5 2.6 %copy.73 = f32[32,16,8,128]{3,2,0,1:T(8,128)} copy(f32[32,16,8,128]{3,1,0,2:T(8,128)S(1)} %convolution_bitcast_fusion.1) | data formatting | bytes 4194304 | tf_op jit(solution)/shard_map/reshape | solution.py:84
  44.1 1.7 %reshape.95 = f32[32,16,1024]{2,0,1:T(8,128)S(1)} reshape(f32[32,16,8,128]{3,2,0,1:T(8,128)} %copy.73) | data formatting | bytes 4194304 | tf_op jit(solution)/shard_map/reshape | solution.py:84
  46.5 0.8 fusion.16
  47.3 1.9 %collective-permute-start = (bf16[16,16,1024]{2,0,1:T(8,128)(2,1)S(1)}, bf16[16,16,1024]{2,0,1:T(8,128)(2,1)S(1)}, u32[]{:S(2)}, u32[]{:S(2)}) collective-permute-start(bf16[16,16,1024]{2,0,1:T(8,128)(2,1)S(1)} %fusion.16), channel_id=1, source_target_pairs={{0,8},{8,16},{16,24},{24,32},{32,40},{40,48},{48,56},{56,64},{64,7... | collective-permute-start | bytes 1572872 | tf_op jit(solution)/shard_map/ppermute | solution.py:17
  49.2 3.8 %collective-permute-start.1 = (bf16[16,16,1024]{2,0,1:T(8,128)(2,1)S(1)}, bf16[16,16,1024]{2,0,1:T(8,128)(2,1)}, u32[]{:S(2)}, u32[]{:S(2)}) collective-permute-start(bf16[16,16,1024]{2,0,1:T(8,128)(2,1)S(1)} %fusion.16), channel_id=1, source_target_pairs={{8,0},{16,8},{24,16},{32,24},{40,32},{48,40},{56,48},{64,56},{72,6... | collective-permute-start | bytes 1572872 | tf_op jit(solution)/shard_map/ppermute | solution.py:19
  53.3 4.5 %collective-permute-done = bf16[16,16,1024]{2,0,1:T(8,128)(2,1)S(1)} collective-permute-done((bf16[16,16,1024]{2,0,1:T(8,128)(2,1)S(1)}, bf16[16,16,1024]{2,0,1:T(8,128)(2,1)S(1)}, u32[]{:S(2)}, u32[]{:S(2)}) %collective-permute-start) | collective-permute-done | bytes 524320 | tf_op jit(solution)/shard_map/ppermute | solution.py:17
  57.8 1.8 %collective-permute-done.1 = bf16[16,16,1024]{2,0,1:T(8,128)(2,1)} collective-permute-done((bf16[16,16,1024]{2,0,1:T(8,128)(2,1)S(1)}, bf16[16,16,1024]{2,0,1:T(8,128)(2,1)}, u32[]{:S(2)}, u32[]{:S(2)}) %collective-permute-start.1) | collective-permute-done | bytes 524320 | tf_op jit(solution)/shard_map/ppermute | solution.py:19
  59.6 1.2 pad_maximum_fusion
  60.8 2.1 %copy.51 = bf16[48,16,1024]{2,1,0:T(8,128)(2,1)} copy(bf16[48,16,1024]{2,0,1:T(8,128)(2,1)S(1)} %pad_maximum_fusion) | data formatting | bytes 3145728
  62.8 48.1 %while.14 = (s32[]{:T(128)}, f32[16,16,1024]{2,1,0:T(8,128)S(1)}, s32[16,16]{0,1:T(8,128)S(1)}, bf16[32,2,1024]{2,0,1:T(8,128)(2,1)S(1)}, s32[16,16]{0,1:T(8,128...) while((s32[]{:T(128)}, f32[16,16,1024]{2,1,0:T(8,128)S(1)}, ...), condition=%wide.region_1.0_spmd.clone, body=%wide.region_0.1_spmd.clone.sunk | while | flops 4195955 | bytes 8524371 | solution.py:115
  62.9 2.0 %gather_fusion = bf16[16,16,1024]{2,1,0:T(8,128)(2,1)S(1)} fusion(bf16[48,16,1024]{2,1,0:T(8,128)(2,1)} %get-tuple-element.285, s32[1024]{0:T(1024)S(1)} %pad_clamp_fusion.4), kind=kCustom, calls=%fused_computation.clone.clone.1 | custom fusion | bytes 1048640 | tf_op jit(solution)/shard_map/while/body/eval_jaxpr/jit(_take)/gather | solution.py:105
  65.9 2.0 %gather_fusion = bf16[16,16,1024]{2,1,0:T(8,128)(2,1)S(1)} fusion(bf16[48,16,1024]{2,1,0:T(8,128)(2,1)} %get-tuple-element.285, s32[1024]{0:T(1024)S(1)} %pad_clamp_fusion.4), kind=kCustom, calls=%fused_computation.clone.clone.1 | custom fusion | bytes 1048640 | tf_op jit(solution)/shard_map/while/body/eval_jaxpr/jit(_take)/gather | solution.py:105
  68.5 0.3 maximum_add_fusion.2
  68.9 2.0 %gather_fusion = bf16[16,16,1024]{2,1,0:T(8,128)(2,1)S(1)} fusion(bf16[48,16,1024]{2,1,0:T(8,128)(2,1)} %get-tuple-element.285, s32[1024]{0:T(1024)S(1)} %pad_clamp_fusion.4), kind=kCustom, calls=%fused_computation.clone.clone.1 | custom fusion | bytes 1048640 | tf_op jit(solution)/shard_map/while/body/eval_jaxpr/jit(_take)/gather | solution.py:105
  71.5 0.3 maximum_add_fusion.2
  71.9 2.0 %gather_fusion = bf16[16,16,1024]{2,1,0:T(8,128)(2,1)S(1)} fusion(bf16[48,16,1024]{2,1,0:T(8,128)(2,1)} %get-tuple-element.285, s32[1024]{0:T(1024)S(1)} %pad_clamp_fusion.4), kind=kCustom, calls=%fused_computation.clone.clone.1 | custom fusion | bytes 1048640 | tf_op jit(solution)/shard_map/while/body/eval_jaxpr/jit(_take)/gather | solution.py:105
  74.5 0.3 maximum_add_fusion.2
  74.9 2.0 %gather_fusion = bf16[16,16,1024]{2,1,0:T(8,128)(2,1)S(1)} fusion(bf16[48,16,1024]{2,1,0:T(8,128)(2,1)} %get-tuple-element.285, s32[1024]{0:T(1024)S(1)} %pad_clamp_fusion.4), kind=kCustom, calls=%fused_computation.clone.clone.1 | custom fusion | bytes 1048640 | tf_op jit(solution)/shard_map/while/body/eval_jaxpr/jit(_take)/gather | solution.py:105
  77.5 0.3 maximum_add_fusion.2
  77.9 2.0 %gather_fusion = bf16[16,16,1024]{2,1,0:T(8,128)(2,1)S(1)} fusion(bf16[48,16,1024]{2,1,0:T(8,128)(2,1)} %get-tuple-element.285, s32[1024]{0:T(1024)S(1)} %pad_clamp_fusion.4), kind=kCustom, calls=%fused_computation.clone.clone.1 | custom fusion | bytes 1048640 | tf_op jit(solution)/shard_map/while/body/eval_jaxpr/jit(_take)/gather | solution.py:105
  80.9 2.0 %gather_fusion = bf16[16,16,1024]{2,1,0:T(8,128)(2,1)S(1)} fusion(bf16[48,16,1024]{2,1,0:T(8,128)(2,1)} %get-tuple-element.285, s32[1024]{0:T(1024)S(1)} %pad_clamp_fusion.4), kind=kCustom, calls=%fused_computation.clone.clone.1 | custom fusion | bytes 1048640 | tf_op jit(solution)/shard_map/while/body/eval_jaxpr/jit(_take)/gather | solution.py:105
  83.5 0.3 maximum_add_fusion.2
  83.9 2.0 %gather_fusion = bf16[16,16,1024]{2,1,0:T(8,128)(2,1)S(1)} fusion(bf16[48,16,1024]{2,1,0:T(8,128)(2,1)} %get-tuple-element.285, s32[1024]{0:T(1024)S(1)} %pad_clamp_fusion.4), kind=kCustom, calls=%fused_computation.clone.clone.1 | custom fusion | bytes 1048640 | tf_op jit(solution)/shard_map/while/body/eval_jaxpr/jit(_take)/gather | solution.py:105
  86.5 0.3 maximum_add_fusion.2
  86.9 2.0 %gather_fusion = bf16[16,16,1024]{2,1,0:T(8,128)(2,1)S(1)} fusion(bf16[48,16,1024]{2,1,0:T(8,128)(2,1)} %get-tuple-element.285, s32[1024]{0:T(1024)S(1)} %pad_clamp_fusion.4), kind=kCustom, calls=%fused_computation.clone.clone.1 | custom fusion | bytes 1048640 | tf_op jit(solution)/shard_map/while/body/eval_jaxpr/jit(_take)/gather | solution.py:105
  89.5 0.3 maximum_add_fusion.2
  89.9 2.0 %gather_fusion = bf16[16,16,1024]{2,1,0:T(8,128)(2,1)S(1)} fusion(bf16[48,16,1024]{2,1,0:T(8,128)(2,1)} %get-tuple-element.285, s32[1024]{0:T(1024)S(1)} %pad_clamp_fusion.4), kind=kCustom, calls=%fused_computation.clone.clone.1 | custom fusion | bytes 1048640 | tf_op jit(solution)/shard_map/while/body/eval_jaxpr/jit(_take)/gather | solution.py:105
  92.5 0.3 maximum_add_fusion.2
  92.9 2.0 %gather_fusion = bf16[16,16,1024]{2,1,0:T(8,128)(2,1)S(1)} fusion(bf16[48,16,1024]{2,1,0:T(8,128)(2,1)} %get-tuple-element.285, s32[1024]{0:T(1024)S(1)} %pad_clamp_fusion.4), kind=kCustom, calls=%fused_computation.clone.clone.1 | custom fusion | bytes 1048640 | tf_op jit(solution)/shard_map/while/body/eval_jaxpr/jit(_take)/gather | solution.py:105
  95.9 2.0 %gather_fusion = bf16[16,16,1024]{2,1,0:T(8,128)(2,1)S(1)} fusion(bf16[48,16,1024]{2,1,0:T(8,128)(2,1)} %get-tuple-element.285, s32[1024]{0:T(1024)S(1)} %pad_clamp_fusion.4), kind=kCustom, calls=%fused_computation.clone.clone.1 | custom fusion | bytes 1048640 | tf_op jit(solution)/shard_map/while/body/eval_jaxpr/jit(_take)/gather | solution.py:105
  98.5 0.3 maximum_add_fusion.2
  98.9 2.0 %gather_fusion = bf16[16,16,1024]{2,1,0:T(8,128)(2,1)S(1)} fusion(bf16[48,16,1024]{2,1,0:T(8,128)(2,1)} %get-tuple-element.285, s32[1024]{0:T(1024)S(1)} %pad_clamp_fusion.4), kind=kCustom, calls=%fused_computation.clone.clone.1 | custom fusion | bytes 1048640 | tf_op jit(solution)/shard_map/while/body/eval_jaxpr/jit(_take)/gather | solution.py:105
  101.5 0.3 maximum_add_fusion.2
  101.9 2.0 %gather_fusion = bf16[16,16,1024]{2,1,0:T(8,128)(2,1)S(1)} fusion(bf16[48,16,1024]{2,1,0:T(8,128)(2,1)} %get-tuple-element.285, s32[1024]{0:T(1024)S(1)} %pad_clamp_fusion.4), kind=kCustom, calls=%fused_computation.clone.clone.1 | custom fusion | bytes 1048640 | tf_op jit(solution)/shard_map/while/body/eval_jaxpr/jit(_take)/gather | solution.py:105
  104.5 0.3 maximum_add_fusion.2
  105.0 2.0 %gather_fusion = bf16[16,16,1024]{2,1,0:T(8,128)(2,1)S(1)} fusion(bf16[48,16,1024]{2,1,0:T(8,128)(2,1)} %get-tuple-element.285, s32[1024]{0:T(1024)S(1)} %pad_clamp_fusion.4), kind=kCustom, calls=%fused_computation.clone.clone.1 | custom fusion | bytes 1048640 | tf_op jit(solution)/shard_map/while/body/eval_jaxpr/jit(_take)/gather | solution.py:105
  107.6 0.3 maximum_add_fusion.2
  108.0 2.0 %gather_fusion = bf16[16,16,1024]{2,1,0:T(8,128)(2,1)S(1)} fusion(bf16[48,16,1024]{2,1,0:T(8,128)(2,1)} %get-tuple-element.285, s32[1024]{0:T(1024)S(1)} %pad_clamp_fusion.4), kind=kCustom, calls=%fused_computation.clone.clone.1 | custom fusion | bytes 1048640 | tf_op jit(solution)/shard_map/while/body/eval_jaxpr/jit(_take)/gather | solution.py:105
  111.0 0.5 fusion.62
  112.8 0.7 convolution_bitcast_fusion
  113.5 4.0 %fusion.19 = bf16[32,16,4,128]{3,2,1,0:T(4,128)(2,1)S(1)} fusion(f32[32,16,8,2,128]{4,1,3,0,2:T(8,128)S(1)} %convolution_bitcast_fusion, s32[8,2]{0,1:T(2,128)S(1)} %copy-done.9), kind=kOutput, calls=%fused_computation.29 | convolution fusion | flops 50593856 | bytes 4718656 | tf_op jit(solution)/shard_map/lcbri,brq->lcqi/dot_general | solution.py:131
  117.5 1.0 convert_element_type.38
  118.6 2.5 %collective-permute-start.2 = (bf16[4,8,128]{2,1,0:T(8,128)(2,1)S(1)}, bf16[4,8,128]{2,1,0:T(8,128)(2,1)S(1)}, u32[]{:S(2)}, u32[]{:S(2)}) collective-permute-start(bf16[4,8,128]{2,1,0:T(8,128)(2,1)S(1)} %copy-done.4), channel_id=1, source_target_pairs={{0,1},{1,2},{2,3},{3,4},{4,5},{5,6},{6,7},{7,8},{8,9},{9,10},{10,1... | collective-permute-start | bytes 24584 | tf_op jit(solution)/shard_map/ppermute | solution.py:17
  121.1 5.2 %collective-permute-start.3 = (bf16[4,8,128]{2,1,0:T(8,128)(2,1)S(1)}, bf16[4,8,128]{2,1,0:T(8,128)(2,1)S(1)}, u32[]{:S(2)}, u32[]{:S(2)}) collective-permute-start(bf16[4,8,128]{2,1,0:T(8,128)(2,1)S(1)} %copy-done.4), channel_id=1, source_target_pairs={{1,0},{2,1},{3,2},{4,3},{5,4},{6,5},{7,6},{8,7},{9,8},{10,9},{11,1... | collective-permute-start | bytes 24584 | tf_op jit(solution)/shard_map/ppermute | solution.py:19
  126.4 1.2 collective-permute-done.3
  127.6 0.6 gather_fusion.2
  128.3 1.6 convolution_bitcast_fusion.7
  129.9 1.6 convolution_bitcast_fusion.3
  131.5 28.1 %reduce-scatter.2.cloned.1.call-done = bf16[4,16,512]{2,1,0:T(8,128)(2,1)} async-done(((bf16[32,16,512]{2,1,0:T(8,128)(2,1)}), bf16[4,16,512]{2,1,0:T(8,128)(2,1)}) %reduce-scatter.2.cloned.1.call-update) | async-done | bytes 65552 | tf_op jit(solution)/shard_map/reduce_scatter | solution.py:132
  159.7 0.8 fusion.91
  161.5 0.8 copy-done.3
  162.3 0.4 fusion.30
  162.7 0.4 fusion.27
  163.1 0.6 pad_maximum_fusion.3
  (179 shorter events, 15.0 us)
Async XLA Ops:
  6.5 34.3 %copy-start = (bf16[8,2,128,128]{3,2,1,0:T(8,128)(2,1)S(1)}, bf16[8,2,128,128]{3,2,1,0:T(8,128)(2,1)}, u32[]{:S(2)}) copy-start(bf16[8,2,128,128]{3,2,1,0:T(8,128)(2,1)} %param.22) | copy-start | bytes 1572868
  6.5 3.4 %copy-start.4 = (bf16[4,8,128]{2,1,0:T(8,128)(2,1)S(1)}, bf16[4,8,128]{2,1,0:T(8,128)(2,1)}, u32[]{:S(2)}) copy-start(bf16[4,8,128]{2,1,0:T(8,128)(2,1)} %param.14) | copy-start | bytes 24580
  6.5 3.4 %copy-start.1 = (bf16[4,2,2,512,128]{4,3,2,1,0:T(8,128)(2,1)S(1)}, bf16[4,2,2,512,128]{4,3,2,1,0:T(8,128)(2,1)}, u32[]{:S(2)}) copy-start(bf16[4,2,2,512,128]{4,3,2,1,0:T(8,128)(2,1)} %param.15) | copy-start | bytes 6291460
  9.9 12.1 %copy-start.9 = (s32[8,2]{0,1:T(2,128)S(1)}, s32[8,2]{0,1:T(2,128)}, u32[]{:S(2)}) copy-start(s32[8,2]{0,1:T(2,128)} %param.21) | copy-start | bytes 196
  10.0 12.3 %copy-start.13 = (s32[32]{0:T(128)S(1)}, s32[32]{0:T(128)}, u32[]{:S(2)}) copy-start(s32[32]{0:T(128)} %param.18) | copy-start | bytes 388
  10.0 12.8 %copy-start.6 = (bf16[8,2,1024]{2,1,0:T(2,128)(2,1)S(1)}, bf16[8,2,1024]{2,1,0:T(2,128)(2,1)}, u32[]{:S(2)}) copy-start(bf16[8,2,1024]{2,1,0:T(2,128)(2,1)} %param.20) | copy-start | bytes 98308
  10.0 12.8 %copy-start.12 = (s32[32]{0:T(128)S(1)}, s32[32]{0:T(128)}, u32[]{:S(2)}) copy-start(s32[32]{0:T(128)} %param.19) | copy-start | bytes 388
  11.7 27.8 %all-to-all-start = ((bf16[8,4,16,512]{3,2,1,0:T(8,128)(2,1)}), bf16[8,4,16,512]{3,2,1,0:T(8,128)(2,1)S(1)}, u32[]{:S(2)}, u32[]{:S(2)}) async-start(bf16[8,4,16,512]{3,2,1,0:T(8,128)(2,1)} %stack.2), calls=%async_computation | async-start | bytes 1048576 | tf_op jit(solution)/shard_map/all_to_all | solution.py:79
  22.0 137.6 %reduce-scatter.2.cloned.1.call-start = ((), (), s32[]{:S(2)}) async-start(), calls=%async_computation.2 | async-start | bytes 589824 | tf_op jit(solution)/shard_map/reduce_scatter | solution.py:132
  45.8 0.7 copy-start.11
  46.1 7.0 %copy-start.5 = (bf16[32,2,1024]{2,1,0:T(2,128)(2,1)S(1)}, bf16[32,2,1024]{2,1,0:T(2,128)(2,1)}, u32[]{:S(2)}) copy-start(bf16[32,2,1024]{2,1,0:T(2,128)(2,1)} %param.25) | copy-start | bytes 393220
  46.1 7.0 %copy-start.7 = (s32[16,16]{1,0:T(8,128)S(1)}, s32[16,16]{1,0:T(8,128)}, u32[]{:S(2)}) copy-start(s32[16,16]{1,0:T(8,128)} %param.24) | copy-start | bytes 3076
  46.2 7.1 %copy-start.8 = (s32[16,16]{1,0:T(8,128)S(1)}, s32[16,16]{1,0:T(8,128)}, u32[]{:S(2)}) copy-start(s32[16,16]{1,0:T(8,128)} %param.23) | copy-start | bytes 3076
  47.3 10.5 %collective-permute-start = (bf16[16,16,1024]{2,0,1:T(8,128)(2,1)S(1)}, bf16[16,16,1024]{2,0,1:T(8,128)(2,1)S(1)}, u32[]{:S(2)}, u32[]{:S(2)}) collective-permute-start(bf16[16,16,1024]{2,0,1:T(8,128)(2,1)S(1)} %fusion.16), channel_id=1, source_target_pairs={{0,8},{8,16},{16,24},{24,32},{32,40},{40,48},{48,56},{56,64},{64,7... | collective-permute-start | bytes 1572872 | tf_op jit(solution)/shard_map/ppermute | solution.py:17
  49.2 10.3 %collective-permute-start.1 = (bf16[16,16,1024]{2,0,1:T(8,128)(2,1)S(1)}, bf16[16,16,1024]{2,0,1:T(8,128)(2,1)}, u32[]{:S(2)}, u32[]{:S(2)}) collective-permute-start(bf16[16,16,1024]{2,0,1:T(8,128)(2,1)S(1)} %fusion.16), channel_id=1, source_target_pairs={{8,0},{16,8},{24,16},{32,24},{40,32},{48,40},{56,48},{64,56},{72,6... | collective-permute-start | bytes 1572872 | tf_op jit(solution)/shard_map/ppermute | solution.py:19
  113.5 12.8 %copy-start.10 = (s32[4,8]{1,0:T(4,128)S(1)}, s32[4,8]{1,0:T(4,128)}, u32[]{:S(2)}) copy-start(s32[4,8]{1,0:T(4,128)} %param.17) | copy-start | bytes 388
  117.5 42.9 %copy-start.2 = (bf16[4,2,2,512,128]{4,3,2,1,0:T(8,128)(2,1)S(1)}, bf16[4,2,2,512,128]{4,3,2,1,0:T(8,128)(2,1)}, u32[]{:S(2)}) copy-start(bf16[4,2,2,512,128]{4,3,2,1,0:T(8,128)(2,1)} %param.15) | copy-start | bytes 6291460
  118.6 7.8 %collective-permute-start.2 = (bf16[4,8,128]{2,1,0:T(8,128)(2,1)S(1)}, bf16[4,8,128]{2,1,0:T(8,128)(2,1)S(1)}, u32[]{:S(2)}, u32[]{:S(2)}) collective-permute-start(bf16[4,8,128]{2,1,0:T(8,128)(2,1)S(1)} %copy-done.4), channel_id=1, source_target_pairs={{0,1},{1,2},{2,3},{3,4},{4,5},{5,6},{6,7},{7,8},{8,9},{9,10},{10,1... | collective-permute-start | bytes 24584 | tf_op jit(solution)/shard_map/ppermute | solution.py:17
  121.1 6.5 %collective-permute-start.3 = (bf16[4,8,128]{2,1,0:T(8,128)(2,1)S(1)}, bf16[4,8,128]{2,1,0:T(8,128)(2,1)S(1)}, u32[]{:S(2)}, u32[]{:S(2)}) collective-permute-start(bf16[4,8,128]{2,1,0:T(8,128)(2,1)S(1)} %copy-done.4), channel_id=1, source_target_pairs={{1,0},{2,1},{3,2},{4,3},{5,4},{6,5},{7,6},{8,7},{9,8},{10,9},{11,1... | collective-permute-start | bytes 24584 | tf_op jit(solution)/shard_map/ppermute | solution.py:19
  160.7 1.6 copy-start.3
Sparse Core Ops, SparseCore 0:
  118.7 40.9 reduce-scatter.1
